TPU v7x, 512 devices: a whole 4x4x16 slice. The times are simulated.
512 devices in a mesh: wide: 64 (over y_lo, z, core), narrow: 8 (over x, y_hi).
Axes of the slice: x: 4, y: 4 (y_hi: 2, y_lo: 2; y = y_hi * 2 + y_lo), z: 16, core: 2. Of those that a mesh axis runs over, the one named last changes fastest.
Arguments:
- cell_rows: bfloat16 [32768, 2048], P('wide', 'narrow'), may hold values from -3 to 3
- attn_gain: float32 [2048], replicated, may hold values from 0.1 to 1.9
- ffn_gain: float32 [2048], replicated, may hold values from 0.1 to 1.9
- panels: bfloat16 [64, 2048, 4096], P('wide', None, 'narrow'), may hold values from -0.125 to 0.125
- panel_slot: int32 [64], replicated, may hold values from 0 to 63, each once
- layout: int32 [256, 3], P('wide'), may hold values from 0 to 31, as said below
Outputs:
- encoded: bfloat16 [32768, 2048], P('wide', 'narrow')
Inputs may be any that keep to these rules, and one draw needn't show every extreme that they name: `panel_slot`: the first three entries name the indices of wide that hold this layer's attention panel, feed-forward input panel and feed-forward output panel; all entries differ. `layout`: row b lists the position p(b) of block b itself first, then two other positions of the same netlist at most 2 away; the three differ. One of the two lies before p(b) and one after it, except for the first two and last two positions of a netlist.
All inputs are finite; a program needn't handle non-finite values.
Results may differ from a plain program's by a relative error of at most 0.018.
Values may be sent and summed in bfloat16 or wider, within the bound.
A program may use at most 64 MiB of HBM per device.

v0:
```python
import jax
import jax.numpy as jnp
from jax import lax
from jax.sharding import PartitionSpec as P

HD = 128
BLK = 128
NET_BLOCKS = 32
epsilon = 1e-05


def spread(block, axis, source):
    block = jnp.where(lax.axis_index(axis) == source, block, jnp.zeros_like(block))
    return lax.psum(block, axis)


def extended(shard, sides, width):
    for axis, dim in sides:
        size, length = (lax.axis_size(axis), shard.shape[dim])
        up = [(i, (i + 1) % size) for i in range(size - 1)]
        down = [(j, i) for i, j in up]
        last = lax.slice_in_dim(shard, length - width, length, axis=dim)
        first = lax.slice_in_dim(shard, 0, width, axis=dim)
        before = lax.ppermute(last, axis, up)
        after = lax.ppermute(first, axis, down)
        shard = jnp.concatenate([before, shard, after], axis=dim)
    return shard


def rms_scale(values, gain):
    mean_square = jnp.mean(values * values, axis=-1, keepdims=True)
    return values * lax.rsqrt(mean_square + epsilon) * gain


def block_mask(layout, query_index):
    wanted = query_index[:, None] + jnp.arange(5, dtype=jnp.int32)[None, :] - 2
    return jnp.any(layout[:, :, None] == wanted[:, None, :], axis=1)


def on_device(cell_rows, attn_gain, ffn_gain, panels, panel_slot, layout):
    attn_panel = spread(panels[0], "wide", panel_slot[0])
    row_count = cell_rows.shape[0]
    block_count = row_count // BLK
    cell_full = lax.all_gather(cell_rows, "narrow", axis=1, tiled=True)
    normed = rms_scale(cell_full.astype(jnp.float32), attn_gain).astype(jnp.bfloat16)
    model_width = attn_panel.shape[0]
    head_count = attn_panel.shape[1] // (4 * HD)
    attn_table = attn_panel.reshape(model_width, head_count, 4, HD)
    projected = jnp.einsum(
        "td,dhjc->thjc", normed, attn_table[:, :, :3, :], preferred_element_type=jnp.float32
    ).astype(jnp.bfloat16)
    key_values = projected[:, :, 1:, :].reshape(row_count, head_count * 2 * HD)
    key_window = extended(key_values, (("wide", 0),), 2 * BLK)
    pair_blocks = key_window.reshape(block_count + 4, BLK, head_count, 2, HD)
    stacked = jnp.stack([pair_blocks[offset : offset + block_count] for offset in range(5)], axis=1)
    query_index = (
        lax.axis_index("wide") * block_count
        + jnp.arange(block_count, dtype=jnp.int32)
        + block_count // 2
    ) % NET_BLOCKS
    allowed = block_mask(layout, query_index)
    queries = projected[:, :, 0, :].reshape(block_count, BLK, head_count, HD)
    scores = jnp.einsum(
        "bqhc,bokhc->bhqok", queries, stacked[:, :, :, :, 0, :], preferred_element_type=jnp.float32
    ) * HD ** (-0.5)
    lifted = jnp.where(allowed[:, None, None, :, None], jnp.exp(scores), jnp.float32(0.0))
    weights = (lifted / jnp.sum(lifted, axis=(3, 4), keepdims=True)).astype(jnp.bfloat16)
    head_out = jnp.einsum(
        "bhqok,bokhc->bqhc", weights, stacked[:, :, :, :, 1, :], preferred_element_type=jnp.float32
    ).astype(jnp.bfloat16)
    head_out = head_out.reshape(row_count, head_count * HD)
    out_rows = attn_table[:, :, 3, :].reshape(model_width, head_count * HD)
    partial_value = lax.dot_general(
        head_out, out_rows, (((1,), (1,)), ((), ())), preferred_element_type=jnp.float32
    )
    attn_part = lax.psum_scatter(
        partial_value.astype(jnp.bfloat16), "narrow", scatter_dimension=1, tiled=True
    ).astype(jnp.float32)
    stream = (cell_rows.astype(jnp.float32) + attn_part).astype(jnp.bfloat16)
    stream_full = lax.all_gather(stream, "narrow", axis=1, tiled=True)
    up_panel = spread(panels[0], "wide", panel_slot[1])
    down_panel = spread(panels[0], "wide", panel_slot[2])
    normed_ffn = rms_scale(stream_full.astype(jnp.float32), ffn_gain).astype(jnp.bfloat16)
    hidden = jax.nn.gelu(
        jnp.dot(normed_ffn, up_panel, preferred_element_type=jnp.float32), approximate=False
    ).astype(jnp.bfloat16)
    ffn_part = lax.dot_general(
        hidden, down_panel, (((1,), (1,)), ((), ())), preferred_element_type=jnp.float32
    )
    mixed_units = lax.psum_scatter(
        ffn_part.astype(jnp.bfloat16), "narrow", scatter_dimension=1, tiled=True
    ).astype(jnp.float32)
    return (stream.astype(jnp.float32) + mixed_units).astype(jnp.bfloat16)


def solution(mesh):
    return jax.shard_map(
        on_device,
        mesh=mesh,
        in_specs=(P("wide", "narrow"), P(), P(), P("wide", None, "narrow"), P(), P("wide", None)),
        out_specs=P("wide", "narrow"),
        check_vma=False,
    )
```

profile of v0, /device:TPU:32, one launch (start us, length us, event | category | flops | bytes accessed | tf_op | source)
XLA Modules:
  0.0 769.4 jit_solution(15220941853354655202)
XLA Ops:
  8.1 1.4 fusion.95
  11.5 4.0 broadcast_select_fusion
  15.4 2.4 copy.23
  17.9 69.8 %all-gather.3.cloned.1.call-done = bf16[512,2048]{1,0:T(8,128)(2,1)} async-done(((bf16[512,256]{1,0:T(8,128)(2,1)}), bf16[512,2048]{1,0:T(8,128)(2,1)}) %all-gather.3.cloned.1.call-update) | async-done | bytes 2097168 | tf_op jit(solution)/shard_map/all_gather | solution.py:44
  87.7 2.1 fusion
  89.8 386.0 %all-reduce.3.cloned.1.call-done = (bf16[2048,512]{1,0:T(8,128)(2,1)}, bf16[2048,512]{1,0:T(8,128)(2,1)}, bf16[2048,1,4,128]{0,3,2,1:T(8,128)(2,1)}) async-done(((bf16[2048,512]{1,0:T(8,128)(2,1)}, bf16[2048,512]{1,0:T(8,128)(2,1)}, bf16[2048,1,4,128]{0,3,2,1:T(8,128)(2,1)}), (bf16[2048,512]{1,0:T(8,128)(2,1)}, bf16[2048,512]{1,0:T(8,128)(2,1)}, ...) | async-done | bytes 6291472 | tf_op jit(solution)/shard_map/psum | solution.py:14
  475.8 1.5 slice.80
  477.3 1.1 fusion.8
  478.6 1.9 collective-permute-start
  480.6 3.6 collective-permute-start.1
  485.0 1.8 collective-permute-done.1
  486.9 0.7 copy_dynamic-update-slice_fusion.3
  487.9 0.7 copy_dynamic-update-slice_fusion.2
  488.6 0.8 constant_dynamic-update-slice_fusion
  489.4 0.7 copy_dynamic-update-slice_fusion.1
  490.9 1.6 fusion.96
  492.9 3.1 convolution_convert_fusion
  496.1 88.7 %reduce-scatter.3.cloned.1.call-done = bf16[512,256]{1,0:T(8,128)(2,1)} async-done(((bf16[512,2048]{1,0:T(8,128)(2,1)}), bf16[512,256]{1,0:T(8,128)(2,1)}) %reduce-scatter.3.cloned.1.call-update) | async-done | bytes 262160 | tf_op jit(solution)/shard_map/reduce_scatter | solution.py:76
  584.8 1.7 add_convert_fusion.1
  586.6 72.5 %all-gather.5.cloned.1.call-done = bf16[512,2048]{1,0:T(8,128)(2,1)} async-done(((bf16[512,256]{1,0:T(8,128)(2,1)}), bf16[512,2048]{1,0:T(8,128)(2,1)}) %all-gather.5.cloned.1.call-update) | async-done | bytes 2097168 | tf_op jit(solution)/shard_map/all_gather | solution.py:80
  659.1 2.2 fusion.3
  661.4 8.1 %convolution_convert_fusion.1 = bf16[512,2048]{1,0:T(8,128)(2,1)} fusion(bf16[2048,512]{1,0:T(8,128)(2,1)} %get-tuple-element.5, bf16[2048,512]{1,0:T(8,128)(2,1)} %get-tuple-element.6, bf16[512,2048]{1,0:T(8,128)(2,1)S(1)} %copy-done.2, f32[2048]{0:T(1024)S(1)} %copy-done.7, f32[512]{0:T(512)S(1)} %add_rsqrt_fusion), kind=kOutput, calls=%fused_computation.11 | convolution fusion | flops 2169765888 | bytes 8398848 | tf_op jit(solution)/shard_map/dot_general | solution.py:87
  669.5 91.0 %reduce-scatter.5.cloned.1.call-done = bf16[512,256]{1,0:T(8,128)(2,1)} async-done(((bf16[512,2048]{1,0:T(8,128)(2,1)}), bf16[512,256]{1,0:T(8,128)(2,1)}) %reduce-scatter.5.cloned.1.call-update) | async-done | bytes 262160 | tf_op jit(solution)/shard_map/reduce_scatter | solution.py:90
  760.5 1.7 add_convert_fusion
  (49 shorter events, 3.5 us)
Async XLA Ops:
  7.4 80.3 %all-gather.3.cloned.1.call-start = ((), (), s32[]{:S(2)}) async-start(), calls=%async_computation.2 | async-start | bytes 2359296 | tf_op jit(solution)/shard_map/all_gather | solution.py:44
  8.1 467.7 %all-reduce.3.cloned.1.call-start = ((), (), s32[]{:S(2)}) async-start(), calls=%async_computation.6 | async-start | bytes 12582912 | tf_op jit(solution)/shard_map/psum | solution.py:14
  17.9 566.9 %reduce-scatter.3.cloned.1.call-start = ((), (), s32[]{:S(2)}) async-start(), calls=%async_computation.3 | async-start | bytes 2359296 | tf_op jit(solution)/shard_map/reduce_scatter | solution.py:76
  89.8 387.5 %copy-start.1 = (bf16[512,2048]{1,0:T(8,128)(2,1)S(1)}, bf16[512,2048]{1,0:T(8,128)(2,1)}, u32[]{:S(2)}) copy-start(bf16[512,2048]{1,0:T(8,128)(2,1)} %all-gather.3.cloned.1.call-done) | copy-start | bytes 6291460
  89.8 387.5 %copy-start.6 = (f32[2048]{0:T(1024)S(1)}, f32[2048]{0:T(1024)}, u32[]{:S(2)}) copy-start(f32[2048]{0:T(1024)} %param.7) | copy-start | bytes 24580
  478.4 6.0 copy-start.5
  478.6 6.4 collective-permute-start
  480.6 6.1 collective-permute-start.1
  490.9 1.6 copy-start.4
  492.9 91.9 %copy-start.3 = (bf16[512,256]{1,0:T(8,128)(2,1)S(1)}, bf16[512,256]{1,0:T(8,128)(2,1)}, u32[]{:S(2)}) copy-start(bf16[512,256]{1,0:T(8,128)(2,1)} %param.6) | copy-start | bytes 786436
  496.1 165.3 %copy-start.7 = (f32[2048]{0:T(1024)S(1)}, f32[2048]{0:T(1024)}, u32[]{:S(2)}) copy-start(f32[2048]{0:T(1024)} %param.8) | copy-start | bytes 24580
  496.1 163.0 %all-gather.5.cloned.1.call-start = ((), (), s32[]{:S(2)}) async-start(), calls=%async_computation.4 | async-start | bytes 2359296 | tf_op jit(solution)/shard_map/all_gather | solution.py:80
  586.5 174.0 %reduce-scatter.5.cloned.1.call-start = ((), (), s32[]{:S(2)}) async-start(), calls=%async_computation.5 | async-start | bytes 2359296 | tf_op jit(solution)/shard_map/reduce_scatter | solution.py:90
  659.1 2.2 copy-start.2
  669.5 91.1 %copy-start = (bf16[512,256]{1,0:T(8,128)(2,1)S(1)}, bf16[512,256]{1,0:T(8,128)(2,1)}, u32[]{:S(2)}) copy-start(bf16[512,256]{1,0:T(8,128)(2,1)} %add_convert_fusion.1) | copy-start | bytes 786436
Sparse Core Ops, SparseCore 0:
  11.2 76.4 all-gather.2
  496.2 88.5 reduce-scatter.2
  587.9 71.1 all-gather.4
  669.6 90.8 reduce-scatter.4
Sparse Core Ops, SparseCore 1:
  18.0 457.7 all-reduce.2
where the time goes:
time: 770 us; the launch traced here: 769 us
  waiting for transfers between devices  710 us (92%)
  between operations  16.7 us (2%)
  matrix products  14.3 us (2%)
  other arithmetic  12 us (2%)
  local copies, waits for them, and re-layouts  10.1 us (1%)
    psum x1, waiting for transfers between devices, spread(): return lax.psum(block, axis)  386 us
    reduce_scatter x1, waiting for transfers between devices, on_device(): lax.psum_scatter(ffn_part.astype(jnp.bfloat16), 'narrow', scatter_dimensi...  91 us
    reduce_scatter x1, waiting for transfers between devices, on_device(): lax.psum_scatter(partial_value.astype(jnp.bfloat16), 'narrow', scatter_di...  88.7 us
    all_gather x1, waiting for transfers between devices, on_device(): stream_full = lax.all_gather(stream, 'narrow', axis=1, tiled=True)  72.5 us
    all_gather x1, waiting for transfers between devices, on_device(): cell_full = lax.all_gather(cell_rows, 'narrow', axis=1, tiled=True)  69.8 us
  transfers between devices with their start and end apart: 7, of which 6 were waited for; matrix products, arithmetic and copies ran while one was open for 1% of the time, Pallas kernels for 0%

commit v1 on v0

--- a/solution.py
+++ b/solution.py
@@ -77,7 +77,15 @@
         partial_value.astype(jnp.bfloat16), "narrow", scatter_dimension=1, tiled=True
     ).astype(jnp.float32)
     stream = (cell_rows.astype(jnp.float32) + attn_part).astype(jnp.bfloat16)
-    stream_full = lax.all_gather(stream, "narrow", axis=1, tiled=True)
+    stream_full = jnp.concatenate(
+        lax.all_to_all(
+            jnp.stack(lax.axis_size("narrow") * [stream], axis=0),
+            axis_name="narrow",
+            split_axis=0,
+            concat_axis=0,
+        ),
+        axis=1,
+    )
     up_panel = spread(panels[0], "wide", panel_slot[1])
     down_panel = spread(panels[0], "wide", panel_slot[2])
     normed_ffn = rms_scale(stream_full.astype(jnp.float32), ffn_gain).astype(jnp.bfloat16)

time: 770 us -> 721 us (0.936)
  waiting for transfers between devices: 710 us -> 638 us
  blocking collectives: 0 us -> 30 us
    all_gather x1 -> x0, waiting for transfers between devices: 72.5 us -> none  [on_device(): stream_full = lax.all_gather(stream, 'narrow', axis=1, tiled=True)]
    all_to_all x0 -> x1, blocking collectives: none -> 30 us  [on_device(): lax.all_to_all(jnp.stack(lax.axis_size('narrow') * [stream], axis=0), axi...]
  transfers between devices with their start and end apart: 7 -> 6, of which waited for: 6 -> 5; matrix products, arithmetic and copies ran while one was open for 1% -> 1% of each run, Pallas kernels for 0% -> 0%
where the time goes in v1:
time: 721 us
  waiting for transfers between devices  638 us (88%)
  blocking collectives  30 us (4%)
  between operations  16.7 us (2%)
  matrix products  13.1 us (2%)
  other arithmetic  10.1 us (1%)
    psum x1, waiting for transfers between devices, spread(): return lax.psum(block, axis)  386 us
    reduce_scatter x1, waiting for transfers between devices, on_device(): lax.psum_scatter(ffn_part.astype(jnp.bfloat16), 'narrow', scatter_dimensi...  90.7 us
    reduce_scatter x1, waiting for transfers between devices, on_device(): lax.psum_scatter(partial_value.astype(jnp.bfloat16), 'narrow', scatter_di...  88.7 us
    all_gather x1, waiting for transfers between devices, on_device(): cell_full = lax.all_gather(cell_rows, 'narrow', axis=1, tiled=True)  69.7 us
    all_to_all x1, blocking collectives, on_device(): lax.all_to_all(jnp.stack(lax.axis_size('narrow') * [stream], axis=0), axi...  30 us
  transfers between devices with their start and end apart: 6, of which 5 were waited for; matrix products, arithmetic and copies ran while one was open for 1% of the time, Pallas kernels for 0%

profile of v1, /device:TPU:32, one launch (start us, length us, event | category | flops | bytes accessed | tf_op | source)
XLA Modules:
  0.0 720.6 jit_solution(12930152803515390527)
XLA Ops:
  7.4 0.7 all-gather.2.cloned.1.call-update
  8.1 1.4 fusion.87
  11.5 4.0 select_bitcast_fusion.1
  15.4 2.4 copy.24
  17.9 69.7 %all-gather.2.cloned.1.call-done = bf16[512,2048]{1,0:T(8,128)(2,1)} async-done(((bf16[512,256]{1,0:T(8,128)(2,1)}), bf16[512,2048]{1,0:T(8,128)(2,1)}) %all-gather.2.cloned.1.call-update) | async-done | bytes 2097168 | tf_op jit(solution)/shard_map/all_gather | solution.py:44
  87.7 2.1 fusion
  89.8 386.0 %all-reduce.3.cloned.1.call-done = (bf16[2048,512]{1,0:T(8,128)(2,1)}, bf16[2048,1,4,128]{0,3,2,1:T(8,128)(2,1)}, bf16[2048,512]{1,0:T(8,128)(2,1)}) async-done(((bf16[2048,512]{1,0:T(8,128)(2,1)}, bf16[2048,1,4,128]{0,3,2,1:T(8,128)(2,1)}, bf16[2048,512]{1,0:T(8,128)(2,1)}), (bf16[2048,512]{1,0:T(8,128)(2,1)}, bf16[2048,1,4,128]{0,3,2,1:T(8,128)(2,1)}, ...) | async-done | bytes 6291472 | tf_op jit(solution)/shard_map/psum | solution.py:14
  475.8 1.5 slice.80
  477.3 1.1 fusion.5
  478.6 1.9 collective-permute-start
  480.6 3.6 collective-permute-start.1
  485.0 1.8 collective-permute-done.1
  487.5 0.4 fusion.88
  487.9 0.4 fusion.11
  488.3 3.1 convolution_convert_fusion
  491.5 88.7 %reduce-scatter.3.cloned.1.call-done = bf16[512,256]{1,0:T(8,128)(2,1)} async-done(((bf16[512,2048]{1,0:T(8,128)(2,1)}), bf16[512,256]{1,0:T(8,128)(2,1)}) %reduce-scatter.3.cloned.1.call-update) | async-done | bytes 262160 | tf_op jit(solution)/shard_map/reduce_scatter | solution.py:76
  580.2 1.0 add_convert_fusion.1
  581.4 0.2 stack.35
  581.6 30.0 %all_to_all.5 = bf16[8,512,256]{1,2,0:T(8,128)(2,1)S(1)} all-to-all(bf16[8,512,256]{1,2,0:T(8,128)(2,1)S(1)} %stack.35), channel_id=1, replica_groups=mesh['wide'=64,'narrow'=8] {'narrow'}, dimensions={0} | all-to-all | bytes 4194304 | tf_op jit(solution)/shard_map/all_to_all | solution.py:81
  611.6 0.5 multiply_reduce_fusion
  612.3 0.5 fusion.4
  612.9 8.1 %convolution_convert_fusion.1 = bf16[512,2048]{1,0:T(8,128)(2,1)} fusion(bf16[2048,512]{1,0:T(8,128)(2,1)} %get-tuple-element.5, bf16[512,2048]{0,1:T(8,128)(2,1)S(1)} %fusion.4, bf16[2048,512]{1,0:T(8,128)(2,1)} %get-tuple-element.7), kind=kOutput, calls=%fused_computation.10 | convolution fusion | flops 2165571584 | bytes 8388608 | tf_op jit(solution)/shard_map/dot_general | solution.py:95
  621.0 90.7 %reduce-scatter.5.cloned.1.call-done = bf16[512,256]{1,0:T(8,128)(2,1)} async-done(((bf16[512,2048]{1,0:T(8,128)(2,1)}), bf16[512,256]{1,0:T(8,128)(2,1)}) %reduce-scatter.5.cloned.1.call-update) | async-done | bytes 262160 | tf_op jit(solution)/shard_map/reduce_scatter | solution.py:98
  711.7 1.7 add_convert_fusion
  (44 shorter events, 2.1 us)
Async XLA Ops:
  7.4 80.3 %all-gather.2.cloned.1.call-start = ((), (), s32[]{:S(2)}) async-start(), calls=%async_computation.3 | async-start | bytes 2359296 | tf_op jit(solution)/shard_map/all_gather | solution.py:44
  8.1 467.7 %all-reduce.3.cloned.1.call-start = ((), (), s32[]{:S(2)}) async-start(), calls=%async_computation.6 | async-start | bytes 12582912 | tf_op jit(solution)/shard_map/psum | solution.py:14
  17.9 562.4 %reduce-scatter.3.cloned.1.call-start = ((), (), s32[]{:S(2)}) async-start(), calls=%async_computation.4 | async-start | bytes 2359296 | tf_op jit(solution)/shard_map/reduce_scatter | solution.py:76
  89.8 387.5 %copy-start = (bf16[512,2048]{1,0:T(8,128)(2,1)S(1)}, bf16[512,2048]{1,0:T(8,128)(2,1)}, u32[]{:S(2)}) copy-start(bf16[512,2048]{1,0:T(8,128)(2,1)} %all-gather.2.cloned.1.call-done) | copy-start | bytes 6291460
  89.8 387.5 %copy-start.4 = (f32[2048]{0:T(1024)S(1)}, f32[2048]{0:T(1024)}, u32[]{:S(2)}) copy-start(f32[2048]{0:T(1024)} %param.7) | copy-start | bytes 24580
  478.4 6.0 copy-start.3
  478.6 6.4 collective-permute-start
  480.6 6.1 collective-permute-start.1
  488.3 91.9 %copy-start.1 = (bf16[512,256]{1,0:T(8,128)(2,1)S(1)}, bf16[512,256]{1,0:T(8,128)(2,1)}, u32[]{:S(2)}) copy-start(bf16[512,256]{1,0:T(8,128)(2,1)} %param.6) | copy-start | bytes 786436
  491.5 220.2 %reduce-scatter.5.cloned.1.call-start = ((), (), s32[]{:S(2)}) async-start(), calls=%async_computation.5 | async-start | bytes 2359296 | tf_op jit(solution)/shard_map/reduce_scatter | solution.py:98
  611.6 0.7 copy-start.2
Sparse Core Ops, SparseCore 0:
  11.2 76.4 all-gather.1
  491.6 88.5 reduce-scatter.2
  621.1 90.5 reduce-scatter.4
Sparse Core Ops, SparseCore 1:
  18.0 457.7 all-reduce.2
